TPU v7x, 128 devices: a whole 4x4x4 slice. The times are simulated.
128 devices in a mesh: req: 4 (over y), exp: 32 (over z, x, core).
Axes of the slice: x: 4, y: 4, z: 4, core: 2. Of those that a mesh axis runs over, the one named last changes fastest.
Arguments:
- hidden: bfloat16 [8, 2048, 2048], P('req', 'exp'), may hold values from -6 to 6
- q_new: bfloat16 [8, 16, 2048, 128], P('req', None, 'exp'), may hold values from -480 to 480
- k_new: bfloat16 [8, 16, 2048, 128], P('req', None, 'exp'), may hold values from -6 to 6
- v_new: bfloat16 [8, 16, 2048, 128], P('req', None, 'exp'), may hold values from -6 to 6
- routes: int32 [8, 2048, 6], P('req', 'exp'), may hold values from 0 to 63, all different within a row; in each aligned block of 64 rows (0 to 63, 64 to 127, ..., all dimensions but the last counted through in order) at most 8 rows name the same one
- slot_request: int32 [8], replicated, may hold values from 0 to 7, each once
- lengths: int32 [8], replicated, may hold values from 5 to 16384, as said below
- cycle_cache: bfloat16 [128, 2, 4096, 128], P(('req', 'exp')), may hold values from -6 to 6
- sink_cache: bfloat16 [128, 2, 4, 128], P(('req', 'exp')), may hold values from -6 to 6
- w_out: bfloat16 [2048, 2048], replicated, may hold values from -0.125 to 0.125
- norm_gain: float32 [2048], replicated, may hold values from 0.5 to 1.5
- router: bfloat16 [2048, 64], replicated, may hold values from -0.125 to 0.125
- w_gate: bfloat16 [2048, 90112], P(None, ('req', 'exp')), may hold values from -0.125 to 0.125
- w_up: bfloat16 [2048, 90112], P(None, ('req', 'exp')), may hold values from -0.125 to 0.125
- w_down: bfloat16 [90112, 2048], P(('req', 'exp')), may hold values from -0.15625 to 0.15625
Outputs:
- layer_out: bfloat16 [8, 2048, 2048], P('req', 'exp')
- cycle_out: bfloat16 [128, 2, 4096, 128], P(('req', 'exp'))
Inputs may be any that keep to these rules, and one draw needn't show every extreme that they name: In every aligned block of 64 rows of routes (the rows of one request on one index of exp) no expert is named by more than 8 rows, a bound that some block reaches. `slot_request`: each request once. `lengths`: some slot has exactly 16384 cached tokens, and some other fewer than 2048.
All inputs are finite; a program needn't handle non-finite values.
Results may differ from a plain program's by a relative error of at most 0.014.
The roundings to bfloat16 on the way count: a program that leaves them out, or rounds other values in their place, can miss the bound.
Values may be sent and summed in bfloat16 or wider, within the bound.
No kernel may reach another device: no remote copies, remote signals or barrier semaphores. Data moves between devices by JAX's collectives and lax.ppermute only.
A program may use at most 192 MiB of HBM per device.

v0:
```python
import math

import jax
import jax.numpy as jnp
from jax import lax
from jax.experimental import pallas as pl
from jax.experimental.pallas import tpu as pltpu
from jax.sharding import PartitionSpec as P


SPLIT = 2
MOST = 8
BLOCK = 512
SINK_PAD = 128
GRAIN = 16
EXPERT_ROWS = 512
CHUNKS = 1


def rotary_tables(length, count, width):
    half_width = width // 2
    frequency = 10000.0 ** (-2.0 * jnp.arange(half_width, dtype=jnp.float32) / width)
    positions = length + jnp.arange(count, dtype=jnp.int32)
    angles = positions.astype(jnp.float32)[:, None] * frequency[None, :]
    cosine = jnp.cos(angles)
    sine = jnp.sin(angles)
    return (
        jnp.concatenate([cosine, cosine], axis=1),
        jnp.concatenate([-sine, sine], axis=1),
    )


def attention_kernel(
    info, arrived, cache, sink, cosine, sine, context, cache_out, k_rot, v_new, scores, shifted, top_acc, sum_acc, out_acc
):
    step = pl.program_id(0)
    length = info[0]
    window = cache.shape[2]
    rows = arrived.shape[2] // 3
    parts = arrived.shape[0]
    seq_len = parts * arrived.shape[1] * rows
    width = arrived.shape[3]
    chunks = BLOCK // (rows * parts)
    turn = lax.rem(length, window)

    def gathered(first_chunk, kind):
        return jnp.concatenate(
            [
                arrived[part, first_chunk + chunk, kind * rows : (kind + 1) * rows, :]
                for chunk in range(chunks)
                for part in range(parts)
            ],
            0,
        )

    def rotated(first_chunk, row_from, kind):
        raw = gathered(first_chunk, kind).astype(jnp.float32)
        cos_rows = cosine[pl.ds(row_from, BLOCK), :]
        sin_rows = sine[pl.ds(row_from, BLOCK), :]
        return raw * cos_rows + pltpu.roll(raw, width // 2, 1) * sin_rows

    @pl.when(step == 0)
    def _():
        for part in range(seq_len // BLOCK):
            k_rot[part * BLOCK : (part + 1) * BLOCK, :] = rotated(
                part * chunks, part * BLOCK, 1
            ).astype(jnp.bfloat16)
            v_new[part * BLOCK : (part + 1) * BLOCK, :] = gathered(part * chunks, 2)
        shift = lax.rem(turn, GRAIN)
        base = turn - shift
        last = lax.rem(base + seq_len, window)
        for kind, fresh in ((0, k_rot), (1, v_new)):
            cache_out[0, kind] = cache[0, kind]
            shifted[0:GRAIN, :] = cache[
                0, kind, pl.ds(pl.multiple_of(base, GRAIN), GRAIN), :
            ].astype(jnp.float32)
            shifted[seq_len : seq_len + GRAIN, :] = cache[
                0, kind, pl.ds(pl.multiple_of(last, GRAIN), GRAIN), :
            ].astype(jnp.float32)
            shifted[pl.ds(shift, seq_len), :] = fresh[...].astype(jnp.float32)

            def place(index, carry):
                target = pl.multiple_of(lax.rem(base + index * GRAIN, window), GRAIN)
                cache_out[0, kind, pl.ds(target, GRAIN), :] = shifted[
                    pl.ds(pl.multiple_of(index * GRAIN, GRAIN), GRAIN), :
                ].astype(jnp.bfloat16)
                return carry

            lax.fori_loop(0, seq_len // GRAIN + 1, place, 0)

    first_row = step * BLOCK
    query = rotated(step * chunks, first_row, 0).astype(jnp.bfloat16)
    row_ids = first_row + lax.broadcasted_iota(jnp.int32, (BLOCK, 1), 0)
    cycle_blocks = window // BLOCK
    new_blocks = seq_len // BLOCK
    sink_block = cycle_blocks + new_blocks
    contract_last = (((1,), (1,)), ((), ()))

    def score(keys):
        return lax.dot_general(query, keys, contract_last, preferred_element_type=jnp.float32)

    def note(block, values):
        best = top_acc[...]
        for lane in range(values.shape[1] // 128):
            best = jnp.maximum(best, values[:, lane * 128 : (lane + 1) * 128])
        top_acc[...] = best
        if values.shape[1] == BLOCK:
            scores[block] = values
        else:
            scores[block, :, 0 : values.shape[1]] = values

    lowest = jnp.float32(-jnp.inf)
    top_acc[...] = jnp.full_like(top_acc, -jnp.inf)

    def order_from(block):
        return lax.rem(block * BLOCK - turn + window, window)

    def cycle_seen(block):
        end = order_from(block) + BLOCK - 1
        return (end > first_row) & (end >= window - length)

    def score_cycle(block, carry):
        start = order_from(block)
        whole = (
            (start + BLOCK <= window)
            & (start > first_row + BLOCK - 1)
            & (start >= window - length)
        )
        keys_at = pl.ds(pl.multiple_of(block * BLOCK, BLOCK), BLOCK)

        @pl.when(whole)
        def _():
            note(block, score(cache[0, 0, keys_at, :]))

        @pl.when(cycle_seen(block) & jnp.logical_not(whole))
        def _():
            order = lax.rem(start + lax.broadcasted_iota(jnp.int32, (1, BLOCK), 1), window)
            order = jnp.where(order >= window - length, order, -1)
            note(block, jnp.where(order > row_ids, score(cache[0, 0, keys_at, :]), lowest))

        return carry

    lax.fori_loop(0, cycle_blocks, score_cycle, 0)

    def score_new(block, carry):
        keys_at = pl.ds(pl.multiple_of(block * BLOCK, BLOCK), BLOCK)
        note(cycle_blocks + block, score(k_rot[keys_at, :]))
        return carry

    lax.fori_loop(0, step, score_new, 0)
    own_at = pl.ds(pl.multiple_of(first_row, BLOCK), BLOCK)
    columns = first_row + lax.broadcasted_iota(jnp.int32, (1, BLOCK), 1)
    note(cycle_blocks + step, jnp.where(columns <= row_ids, score(k_rot[own_at, :]), lowest))
    sink_columns = lax.broadcasted_iota(jnp.int32, (1, SINK_PAD), 1)
    sink_columns = jnp.where(sink_columns < info[1], sink_columns, window + 2 * seq_len + length)
    note(
        sink_block,
        jnp.where(sink_columns <= length + row_ids - window, score(sink[0, 0]), lowest),
    )

    top = jnp.max(top_acc[...], axis=1, keepdims=True)
    factor = jnp.float32(width ** (-0.5) * math.log2(math.e))

    def weights_of(values):
        return jnp.exp2((values - top) * factor)

    def add_up(weights, values):
        total = sum_acc[...]
        for lane in range(weights.shape[1] // 128):
            total = total + weights[:, lane * 128 : (lane + 1) * 128]
        sum_acc[...] = total
        out_acc[...] += jnp.dot(
            weights.astype(jnp.bfloat16), values, preferred_element_type=jnp.float32
        )

    sink_weights = weights_of(scores[sink_block, :, 0:SINK_PAD])
    sum_acc[...] = sink_weights
    out_acc[...] = jnp.dot(
        sink_weights.astype(jnp.bfloat16), sink[0, 1], preferred_element_type=jnp.float32
    )

    def blend_cycle(block, carry):
        @pl.when(cycle_seen(block))
        def _():
            add_up(
                weights_of(scores[block]),
                cache[0, 1, pl.ds(pl.multiple_of(block * BLOCK, BLOCK), BLOCK), :],
            )

        return carry

    lax.fori_loop(0, cycle_blocks, blend_cycle, 0)

    def blend_new(block, carry):
        add_up(
            weights_of(scores[cycle_blocks + block]),
            v_new[pl.ds(pl.multiple_of(block * BLOCK, BLOCK), BLOCK), :],
        )
        return carry

    lax.fori_loop(0, step + 1, blend_new, 0)
    total = jnp.sum(sum_acc[...], axis=1, keepdims=True)
    context[...] = (out_acc[...] / total).astype(jnp.bfloat16)


def attend(info, arrived, cache, sink, cosine, sine, interpret=False):
    groups, senders, rows3, width = arrived.shape
    seq_len = groups * senders * (rows3 // 3)
    window = cache.shape[2]
    block_count = window // BLOCK + seq_len // BLOCK + 1
    once = pl.Buffered(1)
    return pl.pallas_call(
        attention_kernel,
        grid_spec=pltpu.PrefetchScalarGridSpec(
            num_scalar_prefetch=1,
            grid=(seq_len // BLOCK,),
            in_specs=[
                pl.BlockSpec((groups, senders, rows3, width), lambda i, info: (0, 0, 0, 0), pipeline_mode=once),
                pl.BlockSpec((1, 2, window, width), lambda i, info: (0, 0, 0, 0), pipeline_mode=once),
                pl.BlockSpec((1, 2, SINK_PAD, width), lambda i, info: (0, 0, 0, 0), pipeline_mode=once),
                pl.BlockSpec((seq_len, width), lambda i, info: (0, 0), pipeline_mode=once),
                pl.BlockSpec((seq_len, width), lambda i, info: (0, 0), pipeline_mode=once),
            ],
            out_specs=[
                pl.BlockSpec((BLOCK, width), lambda i, info: (i, 0)),
                pl.BlockSpec((1, 2, window, width), lambda i, info: (0, 0, 0, 0), pipeline_mode=once),
            ],
            scratch_shapes=[
                pltpu.VMEM((seq_len, width), jnp.bfloat16),
                pltpu.VMEM((seq_len, width), jnp.bfloat16),
                pltpu.VMEM((block_count, BLOCK, BLOCK), jnp.float32),
                pltpu.VMEM((seq_len + GRAIN, width), jnp.float32),
                pltpu.VMEM((BLOCK, 128), jnp.float32),
                pltpu.VMEM((BLOCK, 128), jnp.float32),
                pltpu.VMEM((BLOCK, width), jnp.float32),
            ],
        ),
        out_shape=[
            jax.ShapeDtypeStruct((seq_len, width), jnp.bfloat16),
            jax.ShapeDtypeStruct(cache.shape, jnp.bfloat16),
        ],
        compiler_params=pltpu.CompilerParams(
            dimension_semantics=("arbitrary",), vmem_limit_bytes=48 << 20
        ),
        interpret=interpret,
        name="attend",
    )(info, arrived, cache, sink, cosine, sine)


def pick_kernel(order, source, target):
    target[...] = source[...]


def pick_rows(order, source):
    block = (1,) + source.shape[1:]
    zeros = (0,) * (source.ndim - 1)
    return pl.pallas_call(
        pick_kernel,
        grid_spec=pltpu.PrefetchScalarGridSpec(
            num_scalar_prefetch=1,
            grid=(order.shape[0],),
            in_specs=[pl.BlockSpec(block, lambda i, order: (order[i],) + zeros)],
            out_specs=pl.BlockSpec(block, lambda i, order: (i,) + zeros),
        ),
        out_shape=jax.ShapeDtypeStruct((order.shape[0],) + source.shape[1:], source.dtype),
        compiler_params=pltpu.CompilerParams(dimension_semantics=("arbitrary",)),
        name="pick_rows",
    )(order, source)


def expert_kernel(
    rows, gate_a, up_a, down_a, gate_b, up_b, down_b, answer, gate_v, up_v, down_v, first, sems
):
    piece = pl.program_id(0)
    block = pl.program_id(1)
    size = rows.shape[0]
    sources = ((gate_a, up_a, down_a), (gate_b, up_b, down_b))

    def copies(number):
        targets = (gate_v.at[number], up_v.at[number], down_v.at[number])
        return [
            pltpu.make_async_copy(source, target, sems.at[number, index])
            for index, (source, target) in enumerate(zip(sources[number], targets))
        ]

    @pl.when((piece == 0) & (block == 0))
    def _():
        for number in range(SPLIT):
            for copy in copies(number):
                copy.start()

    for number in range(SPLIT):

        @pl.when((piece == number) & (block == 0))
        def _():
            for copy in copies(number):
                copy.wait()

    value = rows[...]
    contract_last = (((1,), (1,)), ((), ()))
    gate_part = lax.dot_general(
        value, gate_v[piece], contract_last, preferred_element_type=jnp.float32
    )
    up_part = lax.dot_general(value, up_v[piece], contract_last, preferred_element_type=jnp.float32)
    active = (jax.nn.silu(gate_part) * up_part).astype(jnp.bfloat16)
    output = jnp.dot(active, down_v[piece], preferred_element_type=jnp.float32).astype(jnp.bfloat16)
    at = pl.ds(pl.multiple_of(block * size, size), size)

    @pl.when(piece == 0)
    def _():
        first[at, :] = output

    @pl.when(piece == 1)
    def _():
        answer[...] = (first[at, :].astype(jnp.float32) + output.astype(jnp.float32)).astype(
            jnp.bfloat16
        )


def run_experts(rows, own, other, interpret=False):
    count, model_width = rows.shape
    units = own[0].shape[0]
    size = min(EXPERT_ROWS, count)
    anywhere = pl.BlockSpec(memory_space=pl.ANY)
    return pl.pallas_call(
        expert_kernel,
        grid=(SPLIT, count // size),
        in_specs=[pl.BlockSpec((size, model_width), lambda p, i: (i, 0))] + [anywhere] * 6,
        out_specs=pl.BlockSpec((size, model_width), lambda p, i: (p * i, 0)),
        out_shape=jax.ShapeDtypeStruct(rows.shape, jnp.bfloat16),
        scratch_shapes=[
            pltpu.VMEM((SPLIT, units, model_width), jnp.bfloat16),
            pltpu.VMEM((SPLIT, units, model_width), jnp.bfloat16),
            pltpu.VMEM((SPLIT, units, model_width), jnp.bfloat16),
            pltpu.VMEM(rows.shape, jnp.bfloat16),
            pltpu.SemaphoreType.DMA((SPLIT, 3)),
        ],
        compiler_params=pltpu.CompilerParams(
            dimension_semantics=("arbitrary", "arbitrary"), vmem_limit_bytes=56 << 20
        ),
        interpret=interpret,
        name="run_experts",
    )(rows, *own, *other)


def on_device(
    hidden,
    q_new,
    k_new,
    v_new,
    routes,
    slot_request,
    lengths,
    cycle_cache,
    sink_cache,
    w_out,
    norm_gain,
    router,
    w_gate,
    w_up,
    w_down,
):
    group_width = lax.axis_size("exp")
    group_count = lax.axis_size("req")
    devices_all = group_count * group_width
    group_index = lax.axis_index("req")
    member_index = lax.axis_index("exp")
    slots_here, local_rows, model_width = hidden.shape
    head_count = q_new.shape[1]
    head_dim = q_new.shape[3]
    experts_all = router.shape[1]
    slots_all = slot_request.shape[0]
    seq_len = local_rows * group_width
    tokens = slots_here * local_rows

    held = jnp.clip(slot_request - group_index * slots_here, 0, slots_here - 1)
    source_group = slot_request // slots_here

    def laid_out(part):
        chosen = part[0][None]
        for index in range(1, slots_here):
            flag = (held == index).reshape((slots_all,) + (1,) * (part.ndim - 1))
            chosen = jnp.where(flag, part[index][None], chosen)
        return chosen

    share = local_rows // group_count
    quarters = [
        part.reshape(slots_here, head_count, group_count, share, head_dim)
        for part in (q_new, k_new, v_new)
    ]
    outgoing = jnp.transpose(jnp.concatenate(quarters, axis=3), (2, 0, 1, 3, 4))
    spread = lax.all_to_all(outgoing, "req", split_axis=0, concat_axis=0, tiled=True)
    spread = spread.reshape(slots_all, head_count, 3 * share, head_dim)
    spread = pick_rows(slot_request, spread).reshape(devices_all, 3 * share, head_dim)
    arrived = lax.all_to_all(spread, ("req", "exp"), split_axis=0, concat_axis=0, tiled=True)
    arrived = arrived.reshape(group_count, group_width, 3 * share, head_dim)

    swap = [(index, index ^ 1) for index in range(group_width)]
    own_weights = (w_gate.T, w_up.T, w_down)
    other_weights = tuple(lax.ppermute(part, "exp", swap) for part in own_weights)

    slot_here = group_index * slots_here + member_index // head_count
    length = lax.dynamic_index_in_dim(lengths, slot_here, 0, keepdims=False)
    cosine, sine = rotary_tables(length, seq_len, head_dim)
    sink_count = sink_cache.shape[2]
    sink_padded = jnp.pad(sink_cache, ((0, 0), (0, 0), (0, SINK_PAD - sink_count), (0, 0)))
    info = jnp.stack([length, jnp.int32(sink_count)]).astype(jnp.int32)

    routes_wide = jnp.pad(
        routes.astype(jnp.bfloat16), ((0, 0), (0, 0), (0, 128 - routes.shape[2]))
    )
    states = laid_out(jnp.concatenate([hidden, routes_wide], axis=2))
    states = states.reshape(group_count, tokens, model_width + 128)
    states, arrived, cosine, sine, sink_padded, info, other_weights = lax.optimization_barrier(
        (states, arrived, cosine, sine, sink_padded, info, other_weights)
    )
    states = lax.all_to_all(states, "req", split_axis=0, concat_axis=0, tiled=True)

    def picked_states(states):
        states = states.reshape(group_count, slots_here, local_rows, model_width + 128)
        own_sources = lax.dynamic_slice_in_dim(
            source_group, group_index * slots_here, slots_here
        )
        states = jnp.concatenate(
            [
                lax.dynamic_index_in_dim(states[:, slot], own_sources[slot], 0, keepdims=False)
                for slot in range(slots_here)
            ],
            0,
        )
        hidden_sel = states[:, :model_width]
        route_sel = states[:, model_width : model_width + routes.shape[2]].astype(jnp.int32)
        return hidden_sel, route_sel

    context, cycle_out = attend(info, arrived, cycle_cache, sink_padded, cosine, sine)

    context, states = lax.optimization_barrier((context, states))
    hidden_sel, route_sel = picked_states(states)
    context_rows = lax.all_to_all(
        context.reshape(group_width, local_rows, head_dim),
        "exp",
        split_axis=0,
        concat_axis=0,
        tiled=True,
    ).reshape(slots_here, head_count, local_rows, head_dim)
    context_rows = jnp.transpose(context_rows, (0, 2, 1, 3)).reshape(tokens, head_count * head_dim)
    projected = jnp.dot(context_rows, w_out, preferred_element_type=jnp.float32)
    residual = hidden_sel.astype(jnp.float32) + projected
    inverse = lax.rsqrt(jnp.mean(residual * residual, axis=-1, keepdims=True) + 1e-06)
    normed = (residual * inverse * norm_gain).astype(jnp.bfloat16)

    logits = lax.dot_general(
        router, normed, (((0,), (1,)), ((), ())), preferred_element_type=jnp.float32
    )
    expert_ids = jnp.arange(experts_all, dtype=jnp.int32)
    named = jnp.any(route_sel.T[None] == expert_ids[:, None, None], axis=1)
    token_ids = jnp.arange(tokens, dtype=jnp.int32)
    token_slot = token_ids // local_rows
    before = (token_ids[:, None] < token_ids[None, :]) & (
        token_slot[:, None] == token_slot[None, :]
    )
    ranks = jnp.dot(
        named.astype(jnp.bfloat16), before.astype(jnp.bfloat16), preferred_element_type=jnp.float32
    ).astype(jnp.int32)
    masked = jnp.where(named, logits, -jnp.inf)
    raised = jnp.exp(masked - jnp.max(masked, axis=0, keepdims=True))
    gates = raised / jnp.sum(raised, axis=0, keepdims=True)
    per_chunk = slots_here // CHUNKS
    span = per_chunk * local_rows
    seats = jnp.arange(per_chunk * MOST, dtype=jnp.int32)
    wanted = (token_slot % per_chunk)[None, :] * MOST + ranks
    seated = named[:, None, :] & (wanted[:, None, :] == seats[None, :, None])
    shares = jnp.where(seated, gates[:, None, :], 0.0)
    seats_all = experts_all * per_chunk * MOST

    core_groups = [list(range(core, devices_all, SPLIT)) for core in range(SPLIT)]

    def exchanged(rows):
        return lax.all_to_all(
            rows.reshape(experts_all, per_chunk * MOST, model_width),
            ("req", "exp"),
            split_axis=0,
            concat_axis=0,
            axis_index_groups=core_groups,
            tiled=True,
        ).reshape(seats_all, model_width)

    def slot_part(array, slot):
        return array[..., slot * span : (slot + 1) * span].reshape(seats_all, span)

    def dispatched(slot):
        return jnp.dot(
            slot_part(seated, slot).astype(jnp.bfloat16),
            normed[slot * span : (slot + 1) * span],
            preferred_element_type=jnp.float32,
        ).astype(jnp.bfloat16)

    def combined(slot, returned):
        part = slot_part(shares, slot)
        coarse = lax.reduce_precision(part, 8, 7)
        fine = (part - coarse).astype(jnp.bfloat16)
        both = jnp.concatenate([coarse.astype(jnp.bfloat16), fine], axis=1)
        moe = lax.dot_general(
            both, returned, (((0,), (0,)), ((), ())), preferred_element_type=jnp.float32
        )
        kept = residual[slot * span : (slot + 1) * span]
        return (kept + (moe[:span] + moe[span:])).astype(jnp.bfloat16)

    sent = [dispatched(slot) for slot in range(CHUNKS)]
    received = []
    for slot in range(CHUNKS):
        if slot:
            sent[slot], received[slot - 1] = lax.optimization_barrier(
                (sent[slot], received[slot - 1])
            )
        received.append(exchanged(sent[slot]))
    outputs = []
    for slot in range(CHUNKS):
        answer = run_experts(received[slot], own_weights, other_weights)
        if slot + 1 < CHUNKS:
            answer, received[CHUNKS - 1] = lax.optimization_barrier((answer, received[CHUNKS - 1]))
        outputs.append(exchanged(answer))
    layer_out = jnp.concatenate([combined(slot, outputs[slot]) for slot in range(CHUNKS)])
    layer_out = layer_out.reshape(slots_here, local_rows, model_width)
    return (layer_out, cycle_out)


def solution(mesh):
    in_specs = (
        P("req", "exp", None),
        P("req", None, "exp", None),
        P("req", None, "exp", None),
        P("req", None, "exp", None),
        P("req", "exp", None),
        P(),
        P(),
        P(("req", "exp"), None, None, None),
        P(("req", "exp"), None, None, None),
        P(),
        P(),
        P(),
        P(None, ("req", "exp")),
        P(None, ("req", "exp")),
        P(("req", "exp"), None),
    )
    out_specs = (P("req", "exp", None), P(("req", "exp"), None, None, None))

    return jax.shard_map(
        on_device, mesh=mesh, in_specs=in_specs, out_specs=out_specs, check_vma=False
    )
```

profile of v0, /device:TPU:10, one launch (start us, length us, event | category | flops | bytes accessed | tf_op | source)
XLA Modules:
  0.0 285.6 jit_solution(14940973203473654413)
XLA Ops:
  0.6 2.7 copy_bitcast_fusion
  3.3 5.1 %all-to-all-start = ((bf16[4,2,16,48,128]{4,3,2,1,0:T(8,128)(2,1)}), bf16[4,2,16,48,128]{4,3,2,1,0:T(8,128)(2,1)S(1)}, u32[]{:S(2)}, u32[]{:S(2)}) async-start(bf16[4,2,16,48,128]{4,3,2,1,0:T(8,128)(2,1)} %copy_bitcast_fusion), calls=%async_computation | async-start | bytes 3145728 | tf_op jit(solution)/shard_map/all_to_all | solution.py:392
  11.4 3.7 %fusion.15 = (f32[2048,64]{1,0:T(8,128)S(1)}, f32[2048,64]{1,0:T(8,128)S(1)}, f32[2048,64]{1,0:T(8,128)S(1)}) fusion(f32[64]{0:T(128)S(1)} %multiply_power_fusion, f32[2048]{0:T(1024)S(1)} %add_convert_fusion), kind=kLoop, calls=%fused_computation.36 | loop fusion | flops 262144 | bytes 1581312 | tf_op jit(solution)/shard_map/neg | solution.py:29
  15.1 1.6 pad_maximum_fusion.1
  16.8 10.9 %all-to-all-done = bf16[4,2,16,48,128]{4,3,2,1,0:T(8,128)(2,1)S(1)} async-done(((bf16[4,2,16,48,128]{4,3,2,1,0:T(8,128)(2,1)}), bf16[4,2,16,48,128]{4,3,2,1,0:T(8,128)(2,1)S(1)}, u32[]{:S(2)}, u32[]{:S(2)}) %all-to-all-start) | async-done | bytes 1572896 | tf_op jit(solution)/shard_map/all_to_all | solution.py:392
  27.6 1.1 copy-done.2
  28.8 6.1 %pick_rows.1 = bf16[8,16,48,128]{3,2,1,0:T(8,128)(2,1)} custom-call(s32[8]{0:T(128)} %order.1, bf16[8,16,48,128]{3,2,1,0:T(8,128)(2,1)} %bitcast.81), custom_call_target="tpu_custom_call" | custom-call | tf_op jit(solution)/shard_map/pick_rows/pallas_call | solution.py:257
  34.9 9.4 %all-to-all-start.1 = ((bf16[128,48,128]{2,1,0:T(8,128)(2,1)}), bf16[128,48,128]{2,1,0:T(8,128)(2,1)S(1)}, u32[]{:S(2)}, u32[]{:S(2)}) async-start(bf16[128,48,128]{2,1,0:T(8,128)(2,1)} %bitcast.82), calls=%async_computation.1 | async-start | bytes 3145728 | tf_op jit(solution)/shard_map/all_to_all | solution.py:395
  44.9 1.7 bitcast_select_fusion
  46.6 20.0 %all-to-all-done.1 = bf16[128,48,128]{2,1,0:T(8,128)(2,1)S(1)} async-done(((bf16[128,48,128]{2,1,0:T(8,128)(2,1)}), bf16[128,48,128]{2,1,0:T(8,128)(2,1)S(1)}, u32[]{:S(2)}, u32[]{:S(2)}) %all-to-all-start.1) | async-done | bytes 1572896 | tf_op jit(solution)/shard_map/all_to_all | solution.py:395
  66.7 7.1 %all-to-all-start.2 = ((bf16[4,128,2176]{2,1,0:T(8,128)(2,1)}), bf16[4,128,2176]{2,1,0:T(8,128)(2,1)}, u32[]{:S(2)}, u32[]{:S(2)}) async-start(bf16[4,128,2176]{2,1,0:T(8,128)(2,1)} %bitcast_select_fusion), calls=%async_computation.2 | async-start | bytes 4456448 | tf_op jit(solution)/shard_map/all_to_all | solution.py:417
  78.4 1.2 copy-done.1
  79.6 32.0 %attend.1 = (bf16[2048,128]{1,0:T(8,128)(2,1)}, bf16[1,2,4096,128]{3,2,1,0:T(8,128)(2,1)}) custom-call(s32[2]{0:T(128)S(1)} %pad_add_fusion.info, bf16[4,32,48,128]{3,2,1,0:T(8,128)(2,1)S(1)} %bitcast.75, bf16[1,2,4096,128]{3,2,1,0:T(8,128)(2,1)} %cache.1, bf16[1,2,128,128]{3,2,1,0:T(8,128)(2,1)S(1)} %pad.9.sink, f32[2048,128]{1,0:T(8,128)S(1)} %get-tuple-element.18.cosine, ...), custom_call_target="tpu_custom_call" | custom-call | tf_op jit(solution)/shard_map/attend/pallas_call | solution.py:212
  111.6 5.0 %all-to-all-start.3 = ((bf16[32,64,128]{2,1,0:T(8,128)(2,1)}), bf16[32,64,128]{2,1,0:T(8,128)(2,1)S(1)}, u32[]{:S(2)}, u32[]{:S(2)}) async-start(bf16[32,64,128]{2,1,0:T(8,128)(2,1)} %bitcast.19), calls=%async_computation.3 | async-start | bytes 1048576 | tf_op jit(solution)/shard_map/all_to_all | solution.py:439
  116.6 1.7 fusion.27
  119.0 8.1 %all-to-all-done.3 = bf16[32,64,128]{2,1,0:T(8,128)(2,1)S(1)} async-done(((bf16[32,64,128]{2,1,0:T(8,128)(2,1)}), bf16[32,64,128]{2,1,0:T(8,128)(2,1)S(1)}, u32[]{:S(2)}, u32[]{:S(2)}) %all-to-all-start.3) | async-done | bytes 524320 | tf_op jit(solution)/shard_map/all_to_all | solution.py:439
  127.5 4.8 %multiply_reduce_fusion = (f32[128]{0:T(128)S(1)}, f32[128,2048]{1,0:T(8,128)S(1)}) fusion(bf16[2048,2048]{1,0:T(8,128)(2,1)} %param.24, bf16[16,8,16,128]{3,2,1,0:T(8,128)(2,1)S(1)} %bitcast.83, bf16[64,2176]{1,0:T(8,128)(2,1)S(1)} %dynamic-slice_bitcast_fusion, bf16[64,2176]{1,0:T(8,128)(2,1)S(1)} %dynamic-slice_bitcast_fusion.1), kind=kOutput, calls=%fused_computation.19 | convolution fusion | flops 1075576704 | bytes 10519040 | tf_op jit(solution)/shard_map/dot_general | solution.py:447
  132.3 1.3 convolution_convert_fusion
  133.6 59.3 %all_to_all.30 = bf16[64,16,2048]{2,1,0:T(8,128)(2,1)} all-to-all(bf16[64,16,2048]{2,1,0:T(8,128)(2,1)S(1)} %bitcast.78), channel_id=1, replica_groups={{0,2,4,6,8,10,12,14,16,18,20,22,24,26,28,30,32,34,36,38,40,42,44,46,48,..., dimensions={0} | all-to-all | bytes 8388608 | tf_op jit(solution)/shard_map/all_to_all | solution.py:479
  192.9 28.4 %run_experts.1 = bf16[1024,2048]{1,0:T(8,128)(2,1)} custom-call(bf16[1024,2048]{1,0:T(8,128)(2,1)} %bitcast.77, bf16[704,2048]{1,0:T(8,128)(2,1)} %bitcast.85, bf16[704,2048]{1,0:T(8,128)(2,1)} %bitcast.87, bf16[704,2048]{1,0:T(8,128)(2,1)} %down_a.1, bf16[704,2048]{1,0:T(8,128)(2,1)} %collective-permute-done.gate_b, ...), custom_call_target="tpu_custom_call" | custom-call | tf_op jit(solution)/shard_map/run_experts/pallas_call | solution.py:325
  221.3 9.2 %all-to-all-start.5 = ((bf16[64,16,2048]{2,1,0:T(8,128)(2,1)}), bf16[64,16,2048]{2,1,0:T(8,128)(2,1)}, u32[]{:S(2)}, u32[]{:S(2)}) async-start(bf16[64,16,2048]{2,1,0:T(8,128)(2,1)} %bitcast.76), calls=%async_computation.5 | async-start | bytes 8388608 | tf_op jit(solution)/shard_map/all_to_all | solution.py:479
  231.2 49.9 %all-to-all-done.5 = bf16[64,16,2048]{2,1,0:T(8,128)(2,1)} async-done(((bf16[64,16,2048]{2,1,0:T(8,128)(2,1)}), bf16[64,16,2048]{2,1,0:T(8,128)(2,1)}, u32[]{:S(2)}, u32[]{:S(2)}) %all-to-all-start.5) | async-done | bytes 4194336 | tf_op jit(solution)/shard_map/all_to_all | solution.py:479
  281.1 3.5 %fusion.10 = f32[256,2048]{1,0:T(8,128)S(1)} fusion(bf16[1024,2048]{1,0:T(8,128)(2,1)} %bitcast.30, bf16[1024,128]{1,0:T(8,128)(2,1)S(1)} %get-tuple-element.33, bf16[1024,128]{1,0:T(8,128)(2,1)S(1)} %get-tuple-element.32), kind=kOutput, calls=%fused_computation.29 | convolution fusion | flops 1074790400 | bytes 6815744 | tf_op jit(solution)/shard_map/dot_general | solution.py:503
  284.6 1.0 fusion.4
  (59 shorter events, 5.9 us)
Async XLA Ops:
  0.6 229.9 %copy-start = (bf16[2048,64]{0,1:T(8,128)(2,1)S(1)}, bf16[2048,64]{0,1:T(8,128)(2,1)}, u32[]{:S(2)}) copy-start(bf16[2048,64]{0,1:T(8,128)(2,1)} %param.26) | copy-start | bytes 786436
  3.3 5.6 %copy-start.7 = (s32[8]{0:T(128)S(1)}, s32[8]{0:T(128)}, u32[]{:S(2)}) copy-start(s32[8]{0:T(128)} %order.1) | copy-start | bytes 100
  3.3 5.7 %copy-start.9 = (s32[8]{0:T(128)S(1)}, s32[8]{0:T(128)}, u32[]{:S(2)}) copy-start(s32[8]{0:T(128)} %param.21) | copy-start | bytes 100
  3.3 7.9 %copy-start.5 = (s32[2,64,6]{1,0,2:T(2,128)S(1)}, s32[2,64,6]{1,0,2:T(2,128)}, u32[]{:S(2)}) copy-start(s32[2,64,6]{1,0,2:T(2,128)} %param.19) | copy-start | bytes 9220
  3.3 8.0 %copy-start.6 = (bf16[1,2,4,128]{3,2,1,0:T(4,128)(2,1)S(1)}, bf16[1,2,4,128]{3,2,1,0:T(4,128)(2,1)}, u32[]{:S(2)}) copy-start(bf16[1,2,4,128]{3,2,1,0:T(4,128)(2,1)} %param.23) | copy-start | bytes 6148
  3.3 24.3 %all-to-all-start = ((bf16[4,2,16,48,128]{4,3,2,1,0:T(8,128)(2,1)}), bf16[4,2,16,48,128]{4,3,2,1,0:T(8,128)(2,1)S(1)}, u32[]{:S(2)}, u32[]{:S(2)}) async-start(bf16[4,2,16,48,128]{4,3,2,1,0:T(8,128)(2,1)} %copy_bitcast_fusion), calls=%async_computation | async-start | bytes 3145728 | tf_op jit(solution)/shard_map/all_to_all | solution.py:392
  8.4 58.3 %collective-permute-start = (bf16[704,2048]{1,0:T(8,128)(2,1)}, bf16[704,2048]{1,0:T(8,128)(2,1)}, u32[]{:S(2)}, u32[]{:S(2)}) collective-permute-start(bf16[704,2048]{1,0:T(8,128)(2,1)} %bitcast.84), channel_id=1, source_target_pairs={{0,1},{1,0},{2,3},{3,2},{4,5},{5,4},{6,7},{7,6},{8,9},{9,8},{10,11... | collective-permute-start | bytes 8650760 | tf_op jit(solution)/shard_map/ppermute | solution.py:400
  8.4 58.3 %collective-permute-start.1 = (bf16[704,2048]{1,0:T(8,128)(2,1)}, bf16[704,2048]{1,0:T(8,128)(2,1)}, u32[]{:S(2)}, u32[]{:S(2)}) collective-permute-start(bf16[704,2048]{1,0:T(8,128)(2,1)} %bitcast.86), channel_id=1, source_target_pairs={{0,1},{1,0},{2,3},{3,2},{4,5},{5,4},{6,7},{7,6},{8,9},{9,8},{10,11... | collective-permute-start | bytes 8650760 | tf_op jit(solution)/shard_map/ppermute | solution.py:400
  8.9 57.8 %collective-permute-start.2 = (bf16[704,2048]{1,0:T(8,128)(2,1)}, bf16[704,2048]{1,0:T(8,128)(2,1)}, u32[]{:S(2)}, u32[]{:S(2)}) collective-permute-start(bf16[704,2048]{1,0:T(8,128)(2,1)} %down_a.1), channel_id=1, source_target_pairs={{0,1},{1,0},{2,3},{3,2},{4,5},{5,4},{6,7},{7,6},{8,9},{9,8},{10,11... | collective-permute-start | bytes 8650760 | tf_op jit(solution)/shard_map/ppermute | solution.py:400
  15.1 1.6 copy-start.3
  27.6 1.1 copy-start.2
  34.9 31.7 %all-to-all-start.1 = ((bf16[128,48,128]{2,1,0:T(8,128)(2,1)}), bf16[128,48,128]{2,1,0:T(8,128)(2,1)S(1)}, u32[]{:S(2)}, u32[]{:S(2)}) async-start(bf16[128,48,128]{2,1,0:T(8,128)(2,1)} %bitcast.82), calls=%async_computation.1 | async-start | bytes 3145728 | tf_op jit(solution)/shard_map/all_to_all | solution.py:395
  66.6 7.1 %copy-start.8 = (s32[8]{0:T(128)S(1)}, s32[8]{0:T(128)}, u32[]{:S(2)}) copy-start(s32[8]{0:T(128)} %order.1) | copy-start | bytes 100
  66.7 45.0 %all-to-all-start.2 = ((bf16[4,128,2176]{2,1,0:T(8,128)(2,1)}), bf16[4,128,2176]{2,1,0:T(8,128)(2,1)}, u32[]{:S(2)}, u32[]{:S(2)}) async-start(bf16[4,128,2176]{2,1,0:T(8,128)(2,1)} %bitcast_select_fusion), calls=%async_computation.2 | async-start | bytes 4456448 | tf_op jit(solution)/shard_map/all_to_all | solution.py:417
  78.4 1.2 copy-start.1
  111.6 15.5 %all-to-all-start.3 = ((bf16[32,64,128]{2,1,0:T(8,128)(2,1)}), bf16[32,64,128]{2,1,0:T(8,128)(2,1)S(1)}, u32[]{:S(2)}, u32[]{:S(2)}) async-start(bf16[32,64,128]{2,1,0:T(8,128)(2,1)} %bitcast.19), calls=%async_computation.3 | async-start | bytes 1048576 | tf_op jit(solution)/shard_map/all_to_all | solution.py:439
  127.4 4.8 %copy-start.4 = (f32[2048]{0:T(1024)S(1)}, f32[2048]{0:T(1024)}, u32[]{:S(2)}) copy-start(f32[2048]{0:T(1024)} %param.25) | copy-start | bytes 24580
  221.3 59.8 %all-to-all-start.5 = ((bf16[64,16,2048]{2,1,0:T(8,128)(2,1)}), bf16[64,16,2048]{2,1,0:T(8,128)(2,1)}, u32[]{:S(2)}, u32[]{:S(2)}) async-start(bf16[64,16,2048]{2,1,0:T(8,128)(2,1)} %bitcast.76), calls=%async_computation.5 | async-start | bytes 8388608 | tf_op jit(solution)/shard_map/all_to_all | solution.py:479
where the time goes:
time: 290 us; the launch traced here: 286 us
  waiting for transfers between devices  88.9 us (31%)
  Pallas kernels  66.5 us (23%)
  blocking collectives  59.3 us (20%)
  starting transfers between devices  36.2 us (12%)
  other arithmetic  12.7 us (4%)
  matrix products  10.1 us (3%)
  local copies, waits for them, and re-layouts  6.91 us (2%)
  between operations  4.85 us (2%)
    all_to_all x1, blocking collectives, exchanged(): lax.all_to_all(rows.reshape(experts_all, per_chunk * MOST, model_width),...  59.3 us
    all_to_all x1, waiting for transfers between devices, exchanged(): lax.all_to_all(rows.reshape(experts_all, per_chunk * MOST, model_width),...  49.9 us
    pallas_call x1, Pallas kernels, attend(): pl.pallas_call(attention_kernel, grid_spec=pltpu.PrefetchScalarGridSpec(n...  32 us
    pallas_call x1, Pallas kernels, run_experts(): pl.pallas_call(expert_kernel, grid=(SPLIT, count // size), in_specs=[pl.B...  28.4 us
    all_to_all x1, waiting for transfers between devices, on_device(): lax.all_to_all(spread, ('req', 'exp'), split_axis=0, concat_axis=0, tiled...  20 us
    all_to_all x1, waiting for transfers between devices, on_device(): lax.all_to_all(outgoing, 'req', split_axis=0, concat_axis=0, tiled=True)  10.9 us
    all_to_all x1, starting transfers between devices, on_device(): lax.all_to_all(spread, ('req', 'exp'), split_axis=0, concat_axis=0, tiled...  9.4 us
    all_to_all x1, starting transfers between devices, exchanged(): lax.all_to_all(rows.reshape(experts_all, per_chunk * MOST, model_width),...  9.22 us
  transfers between devices with their start and end apart: 8, of which 4 were waited for; matrix products, arithmetic and copies ran while one was open for 5% of the time, Pallas kernels for 13%

commit v1 on v0

--- a/solution.py
+++ b/solution.py
@@ -247,23 +247,28 @@
     )(info, arrived, cache, sink, cosine, sine)
 
 
-def pick_kernel(order, source, target):
-    target[...] = source[...]
+def pick_kernel(order, source, target, sems):
+    copies = [
+        pltpu.make_async_copy(source.at[order[slot]], target.at[slot], sems.at[slot])
+        for slot in range(target.shape[0])
+    ]
+    for copy in copies:
+        copy.start()
+    for copy in copies:
+        copy.wait()
 
 
 def pick_rows(order, source):
-    block = (1,) + source.shape[1:]
-    zeros = (0,) * (source.ndim - 1)
     return pl.pallas_call(
         pick_kernel,
         grid_spec=pltpu.PrefetchScalarGridSpec(
             num_scalar_prefetch=1,
-            grid=(order.shape[0],),
-            in_specs=[pl.BlockSpec(block, lambda i, order: (order[i],) + zeros)],
-            out_specs=pl.BlockSpec(block, lambda i, order: (i,) + zeros),
+            grid=(1,),
+            in_specs=[pl.BlockSpec(memory_space=pl.ANY)],
+            out_specs=pl.BlockSpec(memory_space=pl.ANY),
+            scratch_shapes=[pltpu.SemaphoreType.DMA((order.shape[0],))],
         ),
         out_shape=jax.ShapeDtypeStruct((order.shape[0],) + source.shape[1:], source.dtype),
-        compiler_params=pltpu.CompilerParams(dimension_semantics=("arbitrary",)),
         name="pick_rows",
     )(order, source)
 
@@ -285,24 +290,32 @@
 
     @pl.when((piece == 0) & (block == 0))
     def _():
+        for copy in copies(0):
+            copy.start()
+
+    def arrive(index):
         for number in range(SPLIT):
-            for copy in copies(number):
-                copy.start()
-
-    for number in range(SPLIT):
-
-        @pl.when((piece == number) & (block == 0))
-        def _():
-            for copy in copies(number):
-                copy.wait()
+
+            @pl.when((piece == number) & (block == 0))
+            def _():
+                copies(number)[index].wait()
 
     value = rows[...]
     contract_last = (((1,), (1,)), ((), ()))
+    arrive(0)
     gate_part = lax.dot_general(
         value, gate_v[piece], contract_last, preferred_element_type=jnp.float32
     )
+    arrive(1)
     up_part = lax.dot_general(value, up_v[piece], contract_last, preferred_element_type=jnp.float32)
     active = (jax.nn.silu(gate_part) * up_part).astype(jnp.bfloat16)
+    arrive(2)
+
+    @pl.when((piece == 0) & (block == 0))
+    def _():
+        for copy in copies(1):
+            copy.start()
+
     output = jnp.dot(active, down_v[piece], preferred_element_type=jnp.float32).astype(jnp.bfloat16)
     at = pl.ds(pl.multiple_of(block * size, size), size)
 
@@ -473,15 +486,12 @@
     shares = jnp.where(seated, gates[:, None, :], 0.0)
     seats_all = experts_all * per_chunk * MOST
 
-    core_groups = [list(range(core, devices_all, SPLIT)) for core in range(SPLIT)]
-
     def exchanged(rows):
         return lax.all_to_all(
-            rows.reshape(experts_all, per_chunk * MOST, model_width),
+            rows.reshape(devices_all, seats_all // devices_all, model_width),
             ("req", "exp"),
             split_axis=0,
             concat_axis=0,
-            axis_index_groups=core_groups,
             tiled=True,
         ).reshape(seats_all, model_width)
 

time: 290 us -> 335 us (1.16)
  Pallas kernels: 66.5 us -> 114 us
    pallas_call x1, Pallas kernels: 6.12 us -> 49.5 us  [pick_rows(): pl.pallas_call(pick_kernel, grid_spec=pltpu.PrefetchScalarGridSpec(num_sc...]
    pallas_call x1, Pallas kernels: 28.4 us -> 32.8 us  [run_experts(): pl.pallas_call(expert_kernel, grid=(SPLIT, count // size), in_specs=[pl.B...]
  transfers between devices with their start and end apart: 8 -> 8, of which waited for: 4 -> 4; matrix products, arithmetic and copies ran while one was open for 5% -> 4% of each run, Pallas kernels for 13% -> 25%
where the time goes in v1:
time: 335 us; the launch traced here: 332 us
  Pallas kernels  114 us (34%)
  waiting for transfers between devices  89.2 us (27%)
  blocking collectives  59.1 us (18%)
  starting transfers between devices  34.4 us (10%)
  other arithmetic  12.7 us (4%)
  matrix products  10.1 us (3%)
  local copies, waits for them, and re-layouts  6.91 us (2%)
  between operations  4.86 us (1%)
    all_to_all x1, blocking collectives, exchanged(): lax.all_to_all(rows.reshape(devices_all, seats_all // devices_all, model_...  59.1 us
    all_to_all x1, waiting for transfers between devices, exchanged(): lax.all_to_all(rows.reshape(devices_all, seats_all // devices_all, model_...  50.2 us
    pallas_call x1, Pallas kernels, pick_rows(): pl.pallas_call(pick_kernel, grid_spec=pltpu.PrefetchScalarGridSpec(num_sc...  49.5 us
    pallas_call x1, Pallas kernels, run_experts(): pl.pallas_call(expert_kernel, grid=(SPLIT, count // size), in_specs=[pl.B...  32.8 us
    pallas_call x1, Pallas kernels, attend(): pl.pallas_call(attention_kernel, grid_spec=pltpu.PrefetchScalarGridSpec(n...  32 us
    all_to_all x1, waiting for transfers between devices, on_device(): lax.all_to_all(spread, ('req', 'exp'), split_axis=0, concat_axis=0, tiled...  20 us
    all_to_all x1, waiting for transfers between devices, on_device(): lax.all_to_all(outgoing, 'req', split_axis=0, concat_axis=0, tiled=True)  10.9 us
    all_to_all x1, starting transfers between devices, on_device(): lax.all_to_all(spread, ('req', 'exp'), split_axis=0, concat_axis=0, tiled...  9.41 us
  transfers between devices with their start and end apart: 8, of which 4 were waited for; matrix products, arithmetic and copies ran while one was open for 4% of the time, Pallas kernels for 25%

profile of v1, /device:TPU:10, one launch (start us, length us, event | category | flops | bytes accessed | tf_op | source)
XLA Modules:
  0.0 331.6 jit_solution(4714354937846816288)
XLA Ops:
  0.6 2.7 copy_bitcast_fusion
  3.3 5.1 %all-to-all-start = ((bf16[4,2,16,48,128]{4,3,2,1,0:T(8,128)(2,1)}), bf16[4,2,16,48,128]{4,3,2,1,0:T(8,128)(2,1)S(1)}, u32[]{:S(2)}, u32[]{:S(2)}) async-start(bf16[4,2,16,48,128]{4,3,2,1,0:T(8,128)(2,1)} %copy_bitcast_fusion), calls=%async_computation | async-start | bytes 3145728 | tf_op jit(solution)/shard_map/all_to_all | solution.py:405
  11.4 3.7 %fusion.16 = (f32[2048,64]{1,0:T(8,128)S(1)}, f32[2048,64]{1,0:T(8,128)S(1)}, f32[2048,64]{1,0:T(8,128)S(1)}) fusion(f32[64]{0:T(128)S(1)} %multiply_power_fusion, f32[2048]{0:T(1024)S(1)} %add_convert_fusion), kind=kLoop, calls=%fused_computation.37 | loop fusion | flops 262144 | bytes 1581312 | tf_op jit(solution)/shard_map/neg | solution.py:29
  15.1 1.6 pad_maximum_fusion.1
  16.8 10.9 %all-to-all-done = bf16[4,2,16,48,128]{4,3,2,1,0:T(8,128)(2,1)S(1)} async-done(((bf16[4,2,16,48,128]{4,3,2,1,0:T(8,128)(2,1)}), bf16[4,2,16,48,128]{4,3,2,1,0:T(8,128)(2,1)S(1)}, u32[]{:S(2)}, u32[]{:S(2)}) %all-to-all-start) | async-done | bytes 1572896 | tf_op jit(solution)/shard_map/all_to_all | solution.py:405
  27.6 1.1 copy-done.2
  28.8 49.5 %pick_rows.1 = bf16[8,16,48,128]{3,2,1,0:T(8,128)(2,1)} custom-call(s32[8]{0:T(128)} %order.1, bf16[8,16,48,128]{3,2,1,0:T(8,128)(2,1)} %bitcast.82), custom_call_target="tpu_custom_call" | custom-call | tf_op jit(solution)/shard_map/pick_rows/pallas_call | solution.py:262
  78.3 9.4 %all-to-all-start.1 = ((bf16[128,48,128]{2,1,0:T(8,128)(2,1)}), bf16[128,48,128]{2,1,0:T(8,128)(2,1)S(1)}, u32[]{:S(2)}, u32[]{:S(2)}) async-start(bf16[128,48,128]{2,1,0:T(8,128)(2,1)} %bitcast.83), calls=%async_computation.1 | async-start | bytes 3145728 | tf_op jit(solution)/shard_map/all_to_all | solution.py:408
  88.3 1.7 bitcast_select_fusion
  90.0 20.0 %all-to-all-done.1 = bf16[128,48,128]{2,1,0:T(8,128)(2,1)S(1)} async-done(((bf16[128,48,128]{2,1,0:T(8,128)(2,1)}), bf16[128,48,128]{2,1,0:T(8,128)(2,1)S(1)}, u32[]{:S(2)}, u32[]{:S(2)}) %all-to-all-start.1) | async-done | bytes 1572896 | tf_op jit(solution)/shard_map/all_to_all | solution.py:408
  110.0 7.1 %all-to-all-start.2 = ((bf16[4,128,2176]{2,1,0:T(8,128)(2,1)}), bf16[4,128,2176]{2,1,0:T(8,128)(2,1)}, u32[]{:S(2)}, u32[]{:S(2)}) async-start(bf16[4,128,2176]{2,1,0:T(8,128)(2,1)} %bitcast_select_fusion), calls=%async_computation.2 | async-start | bytes 4456448 | tf_op jit(solution)/shard_map/all_to_all | solution.py:430
  121.8 1.2 copy-done.1
  123.0 32.0 %attend.1 = (bf16[2048,128]{1,0:T(8,128)(2,1)}, bf16[1,2,4096,128]{3,2,1,0:T(8,128)(2,1)}) custom-call(s32[2]{0:T(128)S(1)} %pad_add_fusion.info, bf16[4,32,48,128]{3,2,1,0:T(8,128)(2,1)S(1)} %bitcast.77, bf16[1,2,4096,128]{3,2,1,0:T(8,128)(2,1)} %cache.1, bf16[1,2,128,128]{3,2,1,0:T(8,128)(2,1)S(1)} %pad.9.sink, f32[2048,128]{1,0:T(8,128)S(1)} %get-tuple-element.18.cosine, ...), custom_call_target="tpu_custom_call" | custom-call | tf_op jit(solution)/shard_map/attend/pallas_call | solution.py:212
  155.0 5.0 %all-to-all-start.3 = ((bf16[32,64,128]{2,1,0:T(8,128)(2,1)}), bf16[32,64,128]{2,1,0:T(8,128)(2,1)S(1)}, u32[]{:S(2)}, u32[]{:S(2)}) async-start(bf16[32,64,128]{2,1,0:T(8,128)(2,1)} %bitcast.19), calls=%async_computation.3 | async-start | bytes 1048576 | tf_op jit(solution)/shard_map/all_to_all | solution.py:452
  160.0 1.7 fusion.28
  162.4 8.1 %all-to-all-done.3 = bf16[32,64,128]{2,1,0:T(8,128)(2,1)S(1)} async-done(((bf16[32,64,128]{2,1,0:T(8,128)(2,1)}), bf16[32,64,128]{2,1,0:T(8,128)(2,1)S(1)}, u32[]{:S(2)}, u32[]{:S(2)}) %all-to-all-start.3) | async-done | bytes 524320 | tf_op jit(solution)/shard_map/all_to_all | solution.py:452
  170.8 4.8 %multiply_reduce_fusion = (f32[128]{0:T(128)S(1)}, f32[128,2048]{1,0:T(8,128)S(1)}) fusion(bf16[2048,2048]{1,0:T(8,128)(2,1)} %param.24, bf16[16,8,16,128]{3,2,1,0:T(8,128)(2,1)S(1)} %bitcast.84, bf16[64,2176]{1,0:T(8,128)(2,1)S(1)} %dynamic-slice_bitcast_fusion, bf16[64,2176]{1,0:T(8,128)(2,1)S(1)} %dynamic-slice_bitcast_fusion.1), kind=kOutput, calls=%fused_computation.21 | convolution fusion | flops 1075576704 | bytes 10519040 | tf_op jit(solution)/shard_map/dot_general | solution.py:460
  175.6 1.3 convert_bitcast_fusion
  177.0 59.1 %all_to_all.30 = bf16[128,8,2048]{2,1,0:T(8,128)(2,1)} all-to-all(bf16[128,8,2048]{2,1,0:T(8,128)(2,1)S(1)} %convert_bitcast_fusion), channel_id=1, replica_groups=mesh['req'=4,'exp'=32] {'req','exp'}, dimensions={0} | all-to-all | bytes 8388608 | tf_op jit(solution)/shard_map/all_to_all | solution.py:490
  236.1 32.8 %run_experts.1 = bf16[1024,2048]{1,0:T(8,128)(2,1)} custom-call(bf16[1024,2048]{1,0:T(8,128)(2,1)} %bitcast.79, bf16[704,2048]{1,0:T(8,128)(2,1)} %bitcast.86, bf16[704,2048]{1,0:T(8,128)(2,1)} %bitcast.88, bf16[704,2048]{1,0:T(8,128)(2,1)} %down_a.1, bf16[704,2048]{1,0:T(8,128)(2,1)} %collective-permute-done.gate_b, ...), custom_call_target="tpu_custom_call" | custom-call | tf_op jit(solution)/shard_map/run_experts/pallas_call | solution.py:338
  268.8 7.3 %all-to-all-start.5 = ((bf16[128,8,2048]{2,1,0:T(8,128)(2,1)}), bf16[128,8,2048]{2,1,0:T(8,128)(2,1)}, u32[]{:S(2)}, u32[]{:S(2)}) async-start(bf16[128,8,2048]{2,1,0:T(8,128)(2,1)} %bitcast.78), calls=%async_computation.5 | async-start | bytes 8388608 | tf_op jit(solution)/shard_map/all_to_all | solution.py:490
  276.9 50.2 %all-to-all-done.5 = bf16[128,8,2048]{2,1,0:T(8,128)(2,1)} async-done(((bf16[128,8,2048]{2,1,0:T(8,128)(2,1)}), bf16[128,8,2048]{2,1,0:T(8,128)(2,1)}, u32[]{:S(2)}, u32[]{:S(2)}) %all-to-all-start.5) | async-done | bytes 4194336 | tf_op jit(solution)/shard_map/all_to_all | solution.py:490
  327.1 3.5 %fusion = f32[256,2048]{1,0:T(8,128)S(1)} fusion(bf16[128,8,2048]{2,1,0:T(8,128)(2,1)} %all-to-all-done.5, bf16[1024,128]{1,0:T(8,128)(2,1)S(1)} %get-tuple-element.33, bf16[1024,128]{1,0:T(8,128)(2,1)S(1)} %get-tuple-element.32), kind=kOutput, calls=%fused_computation | convolution fusion | flops 1074790400 | bytes 6815744 | tf_op jit(solution)/shard_map/dot_general | solution.py:513
  330.5 1.0 fusion.6
  (59 shorter events, 5.9 us)
Async XLA Ops:
  0.6 275.6 %copy-start = (bf16[2048,64]{0,1:T(8,128)(2,1)S(1)}, bf16[2048,64]{0,1:T(8,128)(2,1)}, u32[]{:S(2)}) copy-start(bf16[2048,64]{0,1:T(8,128)(2,1)} %param.26) | copy-start | bytes 786436
  3.3 5.6 %copy-start.7 = (s32[8]{0:T(128)S(1)}, s32[8]{0:T(128)}, u32[]{:S(2)}) copy-start(s32[8]{0:T(128)} %order.1) | copy-start | bytes 100
  3.3 5.7 %copy-start.9 = (s32[8]{0:T(128)S(1)}, s32[8]{0:T(128)}, u32[]{:S(2)}) copy-start(s32[8]{0:T(128)} %param.21) | copy-start | bytes 100
  3.3 7.9 %copy-start.5 = (s32[2,64,6]{1,0,2:T(2,128)S(1)}, s32[2,64,6]{1,0,2:T(2,128)}, u32[]{:S(2)}) copy-start(s32[2,64,6]{1,0,2:T(2,128)} %param.19) | copy-start | bytes 9220
  3.3 8.0 %copy-start.6 = (bf16[1,2,4,128]{3,2,1,0:T(4,128)(2,1)S(1)}, bf16[1,2,4,128]{3,2,1,0:T(4,128)(2,1)}, u32[]{:S(2)}) copy-start(bf16[1,2,4,128]{3,2,1,0:T(4,128)(2,1)} %param.23) | copy-start | bytes 6148
  3.3 24.3 %all-to-all-start = ((bf16[4,2,16,48,128]{4,3,2,1,0:T(8,128)(2,1)}), bf16[4,2,16,48,128]{4,3,2,1,0:T(8,128)(2,1)S(1)}, u32[]{:S(2)}, u32[]{:S(2)}) async-start(bf16[4,2,16,48,128]{4,3,2,1,0:T(8,128)(2,1)} %copy_bitcast_fusion), calls=%async_computation | async-start | bytes 3145728 | tf_op jit(solution)/shard_map/all_to_all | solution.py:405
  8.4 101.6 %collective-permute-start = (bf16[704,2048]{1,0:T(8,128)(2,1)}, bf16[704,2048]{1,0:T(8,128)(2,1)}, u32[]{:S(2)}, u32[]{:S(2)}) collective-permute-start(bf16[704,2048]{1,0:T(8,128)(2,1)} %bitcast.85), channel_id=1, source_target_pairs={{0,1},{1,0},{2,3},{3,2},{4,5},{5,4},{6,7},{7,6},{8,9},{9,8},{10,11... | collective-permute-start | bytes 8650760 | tf_op jit(solution)/shard_map/ppermute | solution.py:413
  8.4 101.6 %collective-permute-start.1 = (bf16[704,2048]{1,0:T(8,128)(2,1)}, bf16[704,2048]{1,0:T(8,128)(2,1)}, u32[]{:S(2)}, u32[]{:S(2)}) collective-permute-start(bf16[704,2048]{1,0:T(8,128)(2,1)} %bitcast.87), channel_id=1, source_target_pairs={{0,1},{1,0},{2,3},{3,2},{4,5},{5,4},{6,7},{7,6},{8,9},{9,8},{10,11... | collective-permute-start | bytes 8650760 | tf_op jit(solution)/shard_map/ppermute | solution.py:413
  8.9 101.1 %collective-permute-start.2 = (bf16[704,2048]{1,0:T(8,128)(2,1)}, bf16[704,2048]{1,0:T(8,128)(2,1)}, u32[]{:S(2)}, u32[]{:S(2)}) collective-permute-start(bf16[704,2048]{1,0:T(8,128)(2,1)} %down_a.1), channel_id=1, source_target_pairs={{0,1},{1,0},{2,3},{3,2},{4,5},{5,4},{6,7},{7,6},{8,9},{9,8},{10,11... | collective-permute-start | bytes 8650760 | tf_op jit(solution)/shard_map/ppermute | solution.py:413
  15.1 1.6 copy-start.3
  27.6 1.1 copy-start.2
  78.3 31.7 %all-to-all-start.1 = ((bf16[128,48,128]{2,1,0:T(8,128)(2,1)}), bf16[128,48,128]{2,1,0:T(8,128)(2,1)S(1)}, u32[]{:S(2)}, u32[]{:S(2)}) async-start(bf16[128,48,128]{2,1,0:T(8,128)(2,1)} %bitcast.83), calls=%async_computation.1 | async-start | bytes 3145728 | tf_op jit(solution)/shard_map/all_to_all | solution.py:408
  110.0 7.1 %copy-start.8 = (s32[8]{0:T(128)S(1)}, s32[8]{0:T(128)}, u32[]{:S(2)}) copy-start(s32[8]{0:T(128)} %order.1) | copy-start | bytes 100
  110.0 45.0 %all-to-all-start.2 = ((bf16[4,128,2176]{2,1,0:T(8,128)(2,1)}), bf16[4,128,2176]{2,1,0:T(8,128)(2,1)}, u32[]{:S(2)}, u32[]{:S(2)}) async-start(bf16[4,128,2176]{2,1,0:T(8,128)(2,1)} %bitcast_select_fusion), calls=%async_computation.2 | async-start | bytes 4456448 | tf_op jit(solution)/shard_map/all_to_all | solution.py:430
  121.8 1.2 copy-start.1
  155.0 15.5 %all-to-all-start.3 = ((bf16[32,64,128]{2,1,0:T(8,128)(2,1)}), bf16[32,64,128]{2,1,0:T(8,128)(2,1)S(1)}, u32[]{:S(2)}, u32[]{:S(2)}) async-start(bf16[32,64,128]{2,1,0:T(8,128)(2,1)} %bitcast.19), calls=%async_computation.3 | async-start | bytes 1048576 | tf_op jit(solution)/shard_map/all_to_all | solution.py:452
  170.8 4.8 %copy-start.4 = (f32[2048]{0:T(1024)S(1)}, f32[2048]{0:T(1024)}, u32[]{:S(2)}) copy-start(f32[2048]{0:T(1024)} %param.25) | copy-start | bytes 24580
  268.8 58.3 %all-to-all-start.5 = ((bf16[128,8,2048]{2,1,0:T(8,128)(2,1)}), bf16[128,8,2048]{2,1,0:T(8,128)(2,1)}, u32[]{:S(2)}, u32[]{:S(2)}) async-start(bf16[128,8,2048]{2,1,0:T(8,128)(2,1)} %bitcast.78), calls=%async_computation.5 | async-start | bytes 8388608 | tf_op jit(solution)/shard_map/all_to_all | solution.py:490

commit v2 on v0

--- a/solution.py
+++ b/solution.py
@@ -248,19 +248,22 @@
 
 
 def pick_kernel(order, source, target):
-    target[...] = source[...]
+    target[0] = source[order[pl.program_id(0)]]
 
 
 def pick_rows(order, source):
-    block = (1,) + source.shape[1:]
     zeros = (0,) * (source.ndim - 1)
     return pl.pallas_call(
         pick_kernel,
         grid_spec=pltpu.PrefetchScalarGridSpec(
             num_scalar_prefetch=1,
             grid=(order.shape[0],),
-            in_specs=[pl.BlockSpec(block, lambda i, order: (order[i],) + zeros)],
-            out_specs=pl.BlockSpec(block, lambda i, order: (i,) + zeros),
+            in_specs=[
+                pl.BlockSpec(
+                    source.shape, lambda i, order: (0,) + zeros, pipeline_mode=pl.Buffered(1)
+                )
+            ],
+            out_specs=pl.BlockSpec((1,) + source.shape[1:], lambda i, order: (i,) + zeros),
         ),
         out_shape=jax.ShapeDtypeStruct((order.shape[0],) + source.shape[1:], source.dtype),
         compiler_params=pltpu.CompilerParams(dimension_semantics=("arbitrary",)),
@@ -285,16 +288,17 @@
 
     @pl.when((piece == 0) & (block == 0))
     def _():
-        for number in range(SPLIT):
-            for copy in copies(number):
-                copy.start()
-
-    for number in range(SPLIT):
-
-        @pl.when((piece == number) & (block == 0))
-        def _():
-            for copy in copies(number):
-                copy.wait()
+        for copy in copies(0):
+            copy.start()
+        for copy in copies(0):
+            copy.wait()
+        for copy in copies(1):
+            copy.start()
+
+    @pl.when((piece == 1) & (block == 0))
+    def _():
+        for copy in copies(1):
+            copy.wait()
 
     value = rows[...]
     contract_last = (((1,), (1,)), ((), ()))
@@ -473,15 +477,12 @@
     shares = jnp.where(seated, gates[:, None, :], 0.0)
     seats_all = experts_all * per_chunk * MOST
 
-    core_groups = [list(range(core, devices_all, SPLIT)) for core in range(SPLIT)]
-
     def exchanged(rows):
         return lax.all_to_all(
-            rows.reshape(experts_all, per_chunk * MOST, model_width),
+            rows.reshape(devices_all, seats_all // devices_all, model_width),
             ("req", "exp"),
             split_axis=0,
             concat_axis=0,
-            axis_index_groups=core_groups,
             tiled=True,
         ).reshape(seats_all, model_width)
 

time: 290 us -> 286 us (0.986)
  no operation moved by 1% of the time
where the time goes in v2:
time: 286 us; the launch traced here: 283 us
  waiting for transfers between devices  89.2 us (31%)
  Pallas kernels  65.3 us (23%)
  blocking collectives  59.1 us (21%)
  starting transfers between devices  34.4 us (12%)
  other arithmetic  12.7 us (4%)
  matrix products  10.1 us (4%)
  local copies, waits for them, and re-layouts  6.91 us (2%)
  between operations  4.85 us (2%)
    all_to_all x1, blocking collectives, exchanged(): lax.all_to_all(rows.reshape(devices_all, seats_all // devices_all, model_...  59.1 us
    all_to_all x1, waiting for transfers between devices, exchanged(): lax.all_to_all(rows.reshape(devices_all, seats_all // devices_all, model_...  50.2 us
    pallas_call x1, Pallas kernels, attend(): pl.pallas_call(attention_kernel, grid_spec=pltpu.PrefetchScalarGridSpec(n...  32 us
    pallas_call x1, Pallas kernels, run_experts(): pl.pallas_call(expert_kernel, grid=(SPLIT, count // size), in_specs=[pl.B...  28.4 us
    all_to_all x1, waiting for transfers between devices, on_device(): lax.all_to_all(spread, ('req', 'exp'), split_axis=0, concat_axis=0, tiled...  20 us
    all_to_all x1, waiting for transfers between devices, on_device(): lax.all_to_all(outgoing, 'req', split_axis=0, concat_axis=0, tiled=True)  10.9 us
    all_to_all x1, starting transfers between devices, on_device(): lax.all_to_all(spread, ('req', 'exp'), split_axis=0, concat_axis=0, tiled...  9.4 us
    all_to_all x1, waiting for transfers between devices, on_device(): lax.all_to_all(context.reshape(group_width, local_rows, head_dim), 'exp',...  8.09 us
  transfers between devices with their start and end apart: 8, of which 4 were waited for; matrix products, arithmetic and copies ran while one was open for 5% of the time, Pallas kernels for 13%

profile of v2, /device:TPU:10, one launch (start us, length us, event | category | flops | bytes accessed | tf_op | source)
XLA Modules:
  0.0 282.6 jit_solution(14382029208449530600)
XLA Ops:
  0.6 2.7 copy_bitcast_fusion
  3.3 5.1 %all-to-all-start = ((bf16[4,2,16,48,128]{4,3,2,1,0:T(8,128)(2,1)}), bf16[4,2,16,48,128]{4,3,2,1,0:T(8,128)(2,1)S(1)}, u32[]{:S(2)}, u32[]{:S(2)}) async-start(bf16[4,2,16,48,128]{4,3,2,1,0:T(8,128)(2,1)} %copy_bitcast_fusion), calls=%async_computation | async-start | bytes 3145728 | tf_op jit(solution)/shard_map/all_to_all | solution.py:396
  11.4 3.7 %fusion.16 = (f32[2048,64]{1,0:T(8,128)S(1)}, f32[2048,64]{1,0:T(8,128)S(1)}, f32[2048,64]{1,0:T(8,128)S(1)}) fusion(f32[64]{0:T(128)S(1)} %multiply_power_fusion, f32[2048]{0:T(1024)S(1)} %add_convert_fusion), kind=kLoop, calls=%fused_computation.37 | loop fusion | flops 262144 | bytes 1581312 | tf_op jit(solution)/shard_map/neg | solution.py:29
  15.1 1.6 pad_maximum_fusion.1
  16.8 10.9 %all-to-all-done = bf16[4,2,16,48,128]{4,3,2,1,0:T(8,128)(2,1)S(1)} async-done(((bf16[4,2,16,48,128]{4,3,2,1,0:T(8,128)(2,1)}), bf16[4,2,16,48,128]{4,3,2,1,0:T(8,128)(2,1)S(1)}, u32[]{:S(2)}, u32[]{:S(2)}) %all-to-all-start) | async-done | bytes 1572896 | tf_op jit(solution)/shard_map/all_to_all | solution.py:396
  27.6 1.1 copy-done.2
  28.8 4.9 %pick_rows.1 = bf16[8,16,48,128]{3,2,1,0:T(8,128)(2,1)} custom-call(s32[8]{0:T(128)} %order.1, bf16[8,16,48,128]{3,2,1,0:T(8,128)(2,1)} %bitcast.82), custom_call_target="tpu_custom_call" | custom-call | tf_op jit(solution)/shard_map/pick_rows/pallas_call | solution.py:256
  33.7 9.4 %all-to-all-start.1 = ((bf16[128,48,128]{2,1,0:T(8,128)(2,1)}), bf16[128,48,128]{2,1,0:T(8,128)(2,1)S(1)}, u32[]{:S(2)}, u32[]{:S(2)}) async-start(bf16[128,48,128]{2,1,0:T(8,128)(2,1)} %bitcast.83), calls=%async_computation.1 | async-start | bytes 3145728 | tf_op jit(solution)/shard_map/all_to_all | solution.py:399
  43.7 1.7 bitcast_select_fusion
  45.4 20.0 %all-to-all-done.1 = bf16[128,48,128]{2,1,0:T(8,128)(2,1)S(1)} async-done(((bf16[128,48,128]{2,1,0:T(8,128)(2,1)}), bf16[128,48,128]{2,1,0:T(8,128)(2,1)S(1)}, u32[]{:S(2)}, u32[]{:S(2)}) %all-to-all-start.1) | async-done | bytes 1572896 | tf_op jit(solution)/shard_map/all_to_all | solution.py:399
  65.5 7.1 %all-to-all-start.2 = ((bf16[4,128,2176]{2,1,0:T(8,128)(2,1)}), bf16[4,128,2176]{2,1,0:T(8,128)(2,1)}, u32[]{:S(2)}, u32[]{:S(2)}) async-start(bf16[4,128,2176]{2,1,0:T(8,128)(2,1)} %bitcast_select_fusion), calls=%async_computation.2 | async-start | bytes 4456448 | tf_op jit(solution)/shard_map/all_to_all | solution.py:421
  77.2 1.2 copy-done.1
  78.4 32.0 %attend.1 = (bf16[2048,128]{1,0:T(8,128)(2,1)}, bf16[1,2,4096,128]{3,2,1,0:T(8,128)(2,1)}) custom-call(s32[2]{0:T(128)S(1)} %pad_add_fusion.info, bf16[4,32,48,128]{3,2,1,0:T(8,128)(2,1)S(1)} %bitcast.77, bf16[1,2,4096,128]{3,2,1,0:T(8,128)(2,1)} %cache.1, bf16[1,2,128,128]{3,2,1,0:T(8,128)(2,1)S(1)} %pad.9.sink, f32[2048,128]{1,0:T(8,128)S(1)} %get-tuple-element.18.cosine, ...), custom_call_target="tpu_custom_call" | custom-call | tf_op jit(solution)/shard_map/attend/pallas_call | solution.py:212
  110.4 5.0 %all-to-all-start.3 = ((bf16[32,64,128]{2,1,0:T(8,128)(2,1)}), bf16[32,64,128]{2,1,0:T(8,128)(2,1)S(1)}, u32[]{:S(2)}, u32[]{:S(2)}) async-start(bf16[32,64,128]{2,1,0:T(8,128)(2,1)} %bitcast.19), calls=%async_computation.3 | async-start | bytes 1048576 | tf_op jit(solution)/shard_map/all_to_all | solution.py:443
  115.5 1.7 fusion.28
  117.8 8.1 %all-to-all-done.3 = bf16[32,64,128]{2,1,0:T(8,128)(2,1)S(1)} async-done(((bf16[32,64,128]{2,1,0:T(8,128)(2,1)}), bf16[32,64,128]{2,1,0:T(8,128)(2,1)S(1)}, u32[]{:S(2)}, u32[]{:S(2)}) %all-to-all-start.3) | async-done | bytes 524320 | tf_op jit(solution)/shard_map/all_to_all | solution.py:443
  126.3 4.8 %multiply_reduce_fusion = (f32[128]{0:T(128)S(1)}, f32[128,2048]{1,0:T(8,128)S(1)}) fusion(bf16[2048,2048]{1,0:T(8,128)(2,1)} %param.24, bf16[16,8,16,128]{3,2,1,0:T(8,128)(2,1)S(1)} %bitcast.84, bf16[64,2176]{1,0:T(8,128)(2,1)S(1)} %dynamic-slice_bitcast_fusion, bf16[64,2176]{1,0:T(8,128)(2,1)S(1)} %dynamic-slice_bitcast_fusion.1), kind=kOutput, calls=%fused_computation.21 | convolution fusion | flops 1075576704 | bytes 10519040 | tf_op jit(solution)/shard_map/dot_general | solution.py:451
  131.1 1.3 convert_bitcast_fusion
  132.4 59.1 %all_to_all.30 = bf16[128,8,2048]{2,1,0:T(8,128)(2,1)} all-to-all(bf16[128,8,2048]{2,1,0:T(8,128)(2,1)S(1)} %convert_bitcast_fusion), channel_id=1, replica_groups=mesh['req'=4,'exp'=32] {'req','exp'}, dimensions={0} | all-to-all | bytes 8388608 | tf_op jit(solution)/shard_map/all_to_all | solution.py:481
  191.5 28.4 %run_experts.1 = bf16[1024,2048]{1,0:T(8,128)(2,1)} custom-call(bf16[1024,2048]{1,0:T(8,128)(2,1)} %bitcast.79, bf16[704,2048]{1,0:T(8,128)(2,1)} %bitcast.86, bf16[704,2048]{1,0:T(8,128)(2,1)} %bitcast.88, bf16[704,2048]{1,0:T(8,128)(2,1)} %down_a.1, bf16[704,2048]{1,0:T(8,128)(2,1)} %collective-permute-done.gate_b, ...), custom_call_target="tpu_custom_call" | custom-call | tf_op jit(solution)/shard_map/run_experts/pallas_call | solution.py:329
  219.9 7.3 %all-to-all-start.5 = ((bf16[128,8,2048]{2,1,0:T(8,128)(2,1)}), bf16[128,8,2048]{2,1,0:T(8,128)(2,1)}, u32[]{:S(2)}, u32[]{:S(2)}) async-start(bf16[128,8,2048]{2,1,0:T(8,128)(2,1)} %bitcast.78), calls=%async_computation.5 | async-start | bytes 8388608 | tf_op jit(solution)/shard_map/all_to_all | solution.py:481
  227.9 50.2 %all-to-all-done.5 = bf16[128,8,2048]{2,1,0:T(8,128)(2,1)} async-done(((bf16[128,8,2048]{2,1,0:T(8,128)(2,1)}), bf16[128,8,2048]{2,1,0:T(8,128)(2,1)}, u32[]{:S(2)}, u32[]{:S(2)}) %all-to-all-start.5) | async-done | bytes 4194336 | tf_op jit(solution)/shard_map/all_to_all | solution.py:481
  278.2 3.5 %fusion = f32[256,2048]{1,0:T(8,128)S(1)} fusion(bf16[128,8,2048]{2,1,0:T(8,128)(2,1)} %all-to-all-done.5, bf16[1024,128]{1,0:T(8,128)(2,1)S(1)} %get-tuple-element.33, bf16[1024,128]{1,0:T(8,128)(2,1)S(1)} %get-tuple-element.32), kind=kOutput, calls=%fused_computation | convolution fusion | flops 1074790400 | bytes 6815744 | tf_op jit(solution)/shard_map/dot_general | solution.py:504
  281.6 1.0 fusion.6
  (59 shorter events, 5.9 us)
Async XLA Ops:
  0.6 226.6 %copy-start = (bf16[2048,64]{0,1:T(8,128)(2,1)S(1)}, bf16[2048,64]{0,1:T(8,128)(2,1)}, u32[]{:S(2)}) copy-start(bf16[2048,64]{0,1:T(8,128)(2,1)} %param.26) | copy-start | bytes 786436
  3.3 5.6 %copy-start.7 = (s32[8]{0:T(128)S(1)}, s32[8]{0:T(128)}, u32[]{:S(2)}) copy-start(s32[8]{0:T(128)} %order.1) | copy-start | bytes 100
  3.3 5.7 %copy-start.9 = (s32[8]{0:T(128)S(1)}, s32[8]{0:T(128)}, u32[]{:S(2)}) copy-start(s32[8]{0:T(128)} %param.21) | copy-start | bytes 100
  3.3 7.9 %copy-start.5 = (s32[2,64,6]{1,0,2:T(2,128)S(1)}, s32[2,64,6]{1,0,2:T(2,128)}, u32[]{:S(2)}) copy-start(s32[2,64,6]{1,0,2:T(2,128)} %param.19) | copy-start | bytes 9220
  3.3 8.0 %copy-start.6 = (bf16[1,2,4,128]{3,2,1,0:T(4,128)(2,1)S(1)}, bf16[1,2,4,128]{3,2,1,0:T(4,128)(2,1)}, u32[]{:S(2)}) copy-start(bf16[1,2,4,128]{3,2,1,0:T(4,128)(2,1)} %param.23) | copy-start | bytes 6148
  3.3 24.3 %all-to-all-start = ((bf16[4,2,16,48,128]{4,3,2,1,0:T(8,128)(2,1)}), bf16[4,2,16,48,128]{4,3,2,1,0:T(8,128)(2,1)S(1)}, u32[]{:S(2)}, u32[]{:S(2)}) async-start(bf16[4,2,16,48,128]{4,3,2,1,0:T(8,128)(2,1)} %copy_bitcast_fusion), calls=%async_computation | async-start | bytes 3145728 | tf_op jit(solution)/shard_map/all_to_all | solution.py:396
  8.4 57.1 %collective-permute-start = (bf16[704,2048]{1,0:T(8,128)(2,1)}, bf16[704,2048]{1,0:T(8,128)(2,1)}, u32[]{:S(2)}, u32[]{:S(2)}) collective-permute-start(bf16[704,2048]{1,0:T(8,128)(2,1)} %bitcast.85), channel_id=1, source_target_pairs={{0,1},{1,0},{2,3},{3,2},{4,5},{5,4},{6,7},{7,6},{8,9},{9,8},{10,11... | collective-permute-start | bytes 8650760 | tf_op jit(solution)/shard_map/ppermute | solution.py:404
  8.4 57.1 %collective-permute-start.1 = (bf16[704,2048]{1,0:T(8,128)(2,1)}, bf16[704,2048]{1,0:T(8,128)(2,1)}, u32[]{:S(2)}, u32[]{:S(2)}) collective-permute-start(bf16[704,2048]{1,0:T(8,128)(2,1)} %bitcast.87), channel_id=1, source_target_pairs={{0,1},{1,0},{2,3},{3,2},{4,5},{5,4},{6,7},{7,6},{8,9},{9,8},{10,11... | collective-permute-start | bytes 8650760 | tf_op jit(solution)/shard_map/ppermute | solution.py:404
  8.9 56.6 %collective-permute-start.2 = (bf16[704,2048]{1,0:T(8,128)(2,1)}, bf16[704,2048]{1,0:T(8,128)(2,1)}, u32[]{:S(2)}, u32[]{:S(2)}) collective-permute-start(bf16[704,2048]{1,0:T(8,128)(2,1)} %down_a.1), channel_id=1, source_target_pairs={{0,1},{1,0},{2,3},{3,2},{4,5},{5,4},{6,7},{7,6},{8,9},{9,8},{10,11... | collective-permute-start | bytes 8650760 | tf_op jit(solution)/shard_map/ppermute | solution.py:404
  15.1 1.6 copy-start.3
  27.6 1.1 copy-start.2
  33.7 31.7 %all-to-all-start.1 = ((bf16[128,48,128]{2,1,0:T(8,128)(2,1)}), bf16[128,48,128]{2,1,0:T(8,128)(2,1)S(1)}, u32[]{:S(2)}, u32[]{:S(2)}) async-start(bf16[128,48,128]{2,1,0:T(8,128)(2,1)} %bitcast.83), calls=%async_computation.1 | async-start | bytes 3145728 | tf_op jit(solution)/shard_map/all_to_all | solution.py:399
  65.5 7.1 %copy-start.8 = (s32[8]{0:T(128)S(1)}, s32[8]{0:T(128)}, u32[]{:S(2)}) copy-start(s32[8]{0:T(128)} %order.1) | copy-start | bytes 100
  65.5 45.0 %all-to-all-start.2 = ((bf16[4,128,2176]{2,1,0:T(8,128)(2,1)}), bf16[4,128,2176]{2,1,0:T(8,128)(2,1)}, u32[]{:S(2)}, u32[]{:S(2)}) async-start(bf16[4,128,2176]{2,1,0:T(8,128)(2,1)} %bitcast_select_fusion), calls=%async_computation.2 | async-start | bytes 4456448 | tf_op jit(solution)/shard_map/all_to_all | solution.py:421
  77.2 1.2 copy-start.1
  110.4 15.5 %all-to-all-start.3 = ((bf16[32,64,128]{2,1,0:T(8,128)(2,1)}), bf16[32,64,128]{2,1,0:T(8,128)(2,1)S(1)}, u32[]{:S(2)}, u32[]{:S(2)}) async-start(bf16[32,64,128]{2,1,0:T(8,128)(2,1)} %bitcast.19), calls=%async_computation.3 | async-start | bytes 1048576 | tf_op jit(solution)/shard_map/all_to_all | solution.py:443
  126.3 4.8 %copy-start.4 = (f32[2048]{0:T(1024)S(1)}, f32[2048]{0:T(1024)}, u32[]{:S(2)}) copy-start(f32[2048]{0:T(1024)} %param.25) | copy-start | bytes 24580
  219.9 58.3 %all-to-all-start.5 = ((bf16[128,8,2048]{2,1,0:T(8,128)(2,1)}), bf16[128,8,2048]{2,1,0:T(8,128)(2,1)}, u32[]{:S(2)}, u32[]{:S(2)}) async-start(bf16[128,8,2048]{2,1,0:T(8,128)(2,1)} %bitcast.78), calls=%async_computation.5 | async-start | bytes 8388608 | tf_op jit(solution)/shard_map/all_to_all | solution.py:481
